TPU v7x, 512 devices: a whole 4x4x16 slice. The times are simulated.
512 devices in a mesh: pair: 64 (over z_lo, x, core), aux: 8 (over y, z_hi).
Axes of the slice: x: 4, y: 4, z: 16 (z_hi: 2, z_lo: 8; z = z_hi * 8 + z_lo), core: 2. Of those that a mesh axis runs over, the one named last changes fastest.
Arguments:
- doubles: bfloat16 [128, 512, 512], P('pair', 'aux'), may hold values from -1.796875 to 1.796875
- singles: bfloat16 [256, 512], replicated, may hold values from -0.8984375 to 0.8984375
- vir_slabs: bfloat16 [4096, 8, 512], P(('aux', 'pair')), may hold values from -0.059814453 to 0.059814453
- occ_slabs: bfloat16 [4096, 256, 512], P(('aux', 'pair')), may hold values from -0.029907227 to 0.029907227
- occ_energy: float32 [256], replicated, may hold values from -2 to -0.5
- vir_energy: float32 [8], replicated, may hold values from 0.1 to 1.5
- pair_list: int32 [128, 2], P('pair'), may hold values from 0 to 255
Outputs:
- new_doubles: float32 [128, 8, 8], P('pair', 'aux')
All inputs are finite; a program needn't handle non-finite values.
Results may differ from a plain program's by a relative error of at most 0.0005.
Values may be sent and summed in bfloat16 or wider, within the bound.
No kernel may reach another device: no remote copies, remote signals or barrier semaphores. Data moves between devices by JAX's collectives and lax.ppermute only.
A program may use at most 64 MiB of HBM per device.

v0:
```python
import math
import jax
import jax.numpy as jnp
from jax import lax
from jax.sharding import PartitionSpec as P

NWIN = 8


def ladder_block(running, slab_block, tau_amps):
    half_done = jnp.einsum(
        "qac,pcd->pqad", slab_block, tau_amps, preferred_element_type=jnp.float32
    ).astype(jnp.bfloat16)
    return running + jnp.einsum(
        "pqad,qbd->pab", half_done, slab_block, preferred_element_type=jnp.float32
    )


def ladder_rows(running, slab_piece, tau_amps):
    row_count = slab_piece.shape[0]
    block_size = math.gcd(row_count, 64)
    blocks = slab_piece.reshape(
        row_count // block_size, block_size, slab_piece.shape[1], slab_piece.shape[2]
    )

    def one_block(carried, slab_block):
        return (ladder_block(carried, slab_block, tau_amps), None)

    return lax.scan(one_block, running, blocks)[0]


def body(doubles, singles, vir_slabs, occ_slabs, occ_energy, vir_energy, pair_list):
    full_doubles = lax.all_gather(doubles, "aux", axis=1, tiled=True)
    first_occ = pair_list[:, 0]
    second_occ = pair_list[:, 1]
    occ_ids = lax.broadcasted_iota(jnp.int32, (pair_list.shape[0], singles.shape[0]), 1)
    match_first = first_occ[:, None] == occ_ids
    match_second = second_occ[:, None] == occ_ids
    row_first = jnp.dot(
        match_first.astype(jnp.bfloat16), singles, preferred_element_type=jnp.float32
    )
    row_second = jnp.dot(
        match_second.astype(jnp.bfloat16), singles, preferred_element_type=jnp.float32
    )
    tau_amps = (
        full_doubles.astype(jnp.float32) + row_first[:, :, None] * row_second[:, None, :]
    ).astype(jnp.bfloat16)
    dressing_cols = singles[:, :NWIN]
    dressed = (
        vir_slabs.astype(jnp.float32)
        - jnp.einsum("ka,qkc->qac", dressing_cols, occ_slabs, preferred_element_type=jnp.float32)
    ).astype(jnp.bfloat16)
    local_pairs = tau_amps.shape[0]
    empty = jnp.zeros((local_pairs, NWIN, NWIN), jnp.float32)
    gathered = lax.all_gather(dressed, "pair", axis=0, tiled=True)
    partial_value = ladder_rows(empty, gathered, tau_amps)
    share = lax.psum_scatter(partial_value, "aux", scatter_dimension=1, tiled=True)
    share_rows = NWIN // lax.axis_size("aux")
    row_start = lax.axis_index("aux") * share_rows
    own_doubles = lax.dynamic_slice_in_dim(full_doubles[:, :NWIN, :NWIN], row_start, share_rows, 1)
    own_vir = lax.dynamic_slice_in_dim(vir_energy, row_start, share_rows, 0)
    energy_first = jnp.sum(jnp.where(match_first, occ_energy[None, :], 0.0), axis=1)
    energy_second = jnp.sum(jnp.where(match_second, occ_energy[None, :], 0.0), axis=1)
    pair_energy = energy_first + energy_second
    denominator = pair_energy[:, None, None] - own_vir[None, :, None] - vir_energy[None, None, :]
    return own_doubles.astype(jnp.float32) + share / denominator


def solution(mesh):
    placed = (
        P("pair", "aux", None),
        P(),
        P(("aux", "pair"), None, None),
        P(("aux", "pair"), None, None),
        P(),
        P(),
        P("pair", None),
    )
    return jax.shard_map(
        body, mesh=mesh, in_specs=placed, out_specs=P("pair", "aux", None), check_vma=False
    )
```

profile of v0, /device:TPU:32, one launch (start us, length us, event | category | flops | bytes accessed | tf_op | source)
XLA Modules:
  0.0 289.2 jit_solution(11236321871546542226)
XLA Ops:
  6.5 0.0 copy-start
  6.5 0.0 all-gather.3.cloned.1.call-start
  6.6 1.8 copy.21
  8.4 0.0 all-gather.3.cloned.1.call-update
  8.4 0.0 all-gather.5.cloned.1.call-start
  8.5 1.9 fusion.13
  10.4 0.0 all-gather.5.cloned.1.call-update
  10.5 0.6 dynamic_slice.11
  11.1 1.3 dynamic-slice
  12.4 0.0 copy-done.2
  12.4 0.2 slice_reduce_fusion.1
  12.6 0.0 copy-done.3
  12.6 0.2 select_reduce_fusion
  12.8 0.6 add_subtract_fusion
  13.5 0.2 fusion.16
  13.7 0.3 fusion.17
  13.9 84.6 %all-gather.3.cloned.1.call-done = bf16[2,512,512]{2,0,1:T(2,128)(2,1)} async-done(((bf16[2,64,512]{2,0,1:T(2,128)(2,1)}), bf16[2,512,512]{2,0,1:T(2,128)(2,1)}) %all-gather.3.cloned.1.call-update) | async-done | bytes 1048592 | tf_op jit(solution)/shard_map/all_gather | solution.py:33
  98.6 2.3 add_convert_fusion
  100.9 0.2 copy.24
  101.1 0.7 slice.16
  101.7 119.4 %all-gather.5.cloned.1.call-done = bf16[512,8,512]{2,1,0:T(8,128)(2,1)} async-done(((bf16[8,8,512]{2,1,0:T(8,128)(2,1)}), bf16[512,8,512]{2,1,0:T(8,128)(2,1)}) %all-gather.5.cloned.1.call-update) | async-done | bytes 4194320 | tf_op jit(solution)/shard_map/all_gather | solution.py:55
  221.1 17.7 %while.11 = (s32[]{:T(128)}, f32[2,8,8]{2,1,0:T(8,128)S(1)}, bf16[8,64,8,512]{3,2,1,0:T(8,128)(2,1)}, bf16[2,512,512]{2,1,0:T(8,128)(2,1)S(1)}, s32[]{:T(128)}, /*index=5*/s32[]{:T(128)}) while((s32[]{:T(128)}, f32[2,8,8]{2,1,0:T(8,128)S(1)}, bf16[8,64,8,512]{3,2,1,0:T(8,128)(2,1)}, bf16[2,512,512]{2,1,0:T(8,128)(2,1)S(1)}, ...), condition=%wide.region_1.2_spmd.clone, body=%wide.region_0.1_spmd.clone.sunk | while | flops 545784064 | bytes 2099279 | solution.py:29
  221.1 2.2 fusion.31
  223.3 2.2 fusion.31
  225.5 2.2 fusion.31
  227.7 2.2 fusion.31
  230.0 2.2 fusion.31
  232.2 2.2 fusion.31
  234.4 2.2 fusion.31
  236.6 2.2 fusion.31
  238.8 42.2 %all-reduce = f32[2,8,8]{2,0,1:T(2,128)S(1)} all-reduce(f32[2,8,8]{2,0,1:T(2,128)S(1)} %copy.25), channel_id=2, replica_groups=mesh['pair'=64,'aux'=8] {'aux'}, use_global_device_ids=true, to_apply=%region_2.3.clone | all-reduce | flops 128 | bytes 1024
  281.1 1.3 fusion.20
  (9 shorter events, 0.0 us)
Async XLA Ops:
  6.5 2.0 copy-start
  6.5 6.9 %copy-start.1 = (bf16[256,512]{1,0:T(8,128)(2,1)S(1)}, bf16[256,512]{1,0:T(8,128)(2,1)}, u32[]{:S(2)}) copy-start(bf16[256,512]{1,0:T(8,128)(2,1)} %param.10) | copy-start | bytes 786436
  6.5 3.9 %copy-start.4 = (f32[8]{0:T(128)S(1)}, f32[8]{0:T(128)}, u32[]{:S(2)}) copy-start(f32[8]{0:T(128)} %param.14) | copy-start | bytes 100
  6.5 5.9 %copy-start.2 = (s32[2,2]{1,0:T(2,128)S(1)}, s32[2,2]{1,0:T(2,128)}, u32[]{:S(2)}) copy-start(s32[2,2]{1,0:T(2,128)} %param.15) | copy-start | bytes 52
  6.5 6.1 %copy-start.3 = (f32[256]{0:T(256)S(1)}, f32[256]{0:T(256)}, u32[]{:S(2)}) copy-start(f32[256]{0:T(256)} %param.13) | copy-start | bytes 3076
  6.5 92.0 %all-gather.3.cloned.1.call-start = ((), (), s32[]{:S(2)}) async-start(), calls=%async_computation | async-start | bytes 1179648 | tf_op jit(solution)/shard_map/all_gather | solution.py:33
  8.4 212.7 %all-gather.5.cloned.1.call-start = ((), (), s32[]{:S(2)}) async-start(), calls=%async_computation.1 | async-start | bytes 4259840 | tf_op jit(solution)/shard_map/all_gather | solution.py:55
Sparse Core Ops, SparseCore 0:
  10.6 87.9 all-gather.2
  100.7 120.3 all-gather.4
where the time goes:
time: 290 us; the launch traced here: 289 us
  waiting for transfers between devices  204 us (70%)
  blocking collectives  42.2 us (15%)
  matrix products  19.9 us (7%)
  between operations  13.5 us (5%)
  local copies, waits for them, and re-layouts  4.82 us (2%)
  other arithmetic  4.42 us (2%)
    all_gather x1, waiting for transfers between devices, body(): gathered = lax.all_gather(dressed, 'pair', axis=0, tiled=True)  119 us
    all_gather x1, waiting for transfers between devices, body(): full_doubles = lax.all_gather(doubles, 'aux', axis=1, tiled=True)  84.6 us
    unnamed x1, blocking collectives  42.2 us
    dot_general x8, matrix products, ladder_block(): jnp.einsum('pqad,qbd->pab', half_done, slab_block, preferred_element_type...  17.5 us
  transfers between devices with their start and end apart: 2, of which 2 were waited for; matrix products, arithmetic and copies ran while one was open for 3% of the time, Pallas kernels for 0%

commit v1 on v0

--- a/solution.py
+++ b/solution.py
@@ -5,6 +5,11 @@
 from jax.sharding import PartitionSpec as P
 
 NWIN = 8
+
+
+def gather_over(x, axis, dim):
+    repeated = jnp.stack([x] * lax.axis_size(axis))
+    return jnp.concatenate(lax.all_to_all(repeated, axis, 0, 0), axis=dim)
 
 
 def ladder_block(running, slab_block, tau_amps):
@@ -30,7 +35,7 @@
 
 
 def body(doubles, singles, vir_slabs, occ_slabs, occ_energy, vir_energy, pair_list):
-    full_doubles = lax.all_gather(doubles, "aux", axis=1, tiled=True)
+    full_doubles = gather_over(doubles, "aux", 1)
     first_occ = pair_list[:, 0]
     second_occ = pair_list[:, 1]
     occ_ids = lax.broadcasted_iota(jnp.int32, (pair_list.shape[0], singles.shape[0]), 1)

time: 290 us -> 243 us (0.84)
  the two profiles are of different devices: /device:TPU:32 before, /device:TPU:36 now
where the time goes in v1:
time: 243 us
  waiting for transfers between devices  142 us (58%)
  blocking collectives  43 us (18%)
  matrix products  19.8 us (8%)
  starting transfers between devices  16.8 us (7%)
  between operations  13.5 us (6%)
  local copies, waits for them, and re-layouts  4.83 us (2%)
    all_gather x1, waiting for transfers between devices, body(): gathered = lax.all_gather(dressed, 'pair', axis=0, tiled=True)  87.2 us
    all_to_all x1, waiting for transfers between devices, gather_over(): return jnp.concatenate(lax.all_to_all(repeated, axis, 0, 0), axis=dim)  54.8 us
    unnamed x1, blocking collectives  43 us
    dot_general x8, matrix products, ladder_block(): jnp.einsum('pqad,qbd->pab', half_done, slab_block, preferred_element_type...  17.5 us
    all_to_all x1, starting transfers between devices, gather_over(): return jnp.concatenate(lax.all_to_all(repeated, axis, 0, 0), axis=dim)  16.8 us
  transfers between devices with their start and end apart: 2, of which 2 were waited for; matrix products, arithmetic and copies ran while one was open for 2% of the time, Pallas kernels for 0%

profile of v1, /device:TPU:36, one launch (start us, length us, event | category | flops | bytes accessed | tf_op | source)
XLA Modules:
  0.0 242.6 jit_solution(7728252992855049520)
XLA Ops:
  6.5 0.0 copy-start
  6.5 0.0 all-gather.2.cloned.1.call-start
  6.5 1.6 copy-done
  8.1 1.9 fusion.13
  10.1 0.0 all-gather.2.cloned.1.call-update
  10.1 0.0 copy-done.1
  10.1 1.1 stack.2
  11.2 16.8 %all-to-all-start = ((bf16[8,2,64,512]{3,2,1,0:T(8,128)(2,1)}), bf16[8,2,64,512]{3,2,1,0:T(8,128)(2,1)S(1)}, u32[]{:S(2)}, u32[]{:S(2)}) async-start(bf16[8,2,64,512]{3,2,1,0:T(8,128)(2,1)} %stack.2), calls=%async_computation | async-start | bytes 2097152 | tf_op jit(solution)/shard_map/all_to_all | solution.py:12
  28.0 0.0 copy-done.5
  28.0 0.6 dynamic_slice.11
  28.6 1.3 dynamic-slice
  29.9 0.0 copy-done.3
  29.9 0.2 slice_reduce_fusion.1
  30.1 0.2 select_reduce_fusion
  30.3 0.6 add_subtract_fusion
  30.9 0.2 fusion.16
  31.1 0.2 fusion.17
  31.3 54.8 %all-to-all-done = bf16[8,2,64,512]{3,2,1,0:T(8,128)(2,1)S(1)} async-done(((bf16[8,2,64,512]{3,2,1,0:T(8,128)(2,1)}), bf16[8,2,64,512]{3,2,1,0:T(8,128)(2,1)S(1)}, u32[]{:S(2)}, u32[]{:S(2)}) %all-to-all-start) | async-done | bytes 1048608 | tf_op jit(solution)/shard_map/all_to_all | solution.py:12
  86.2 0.1 copy.22
  86.3 0.3 add_convert_fusion
  86.6 87.2 %all-gather.2.cloned.1.call-done = bf16[512,8,512]{2,1,0:T(8,128)(2,1)} async-done(((bf16[8,8,512]{2,1,0:T(8,128)(2,1)}), bf16[512,8,512]{2,1,0:T(8,128)(2,1)}) %all-gather.2.cloned.1.call-update) | async-done | bytes 4194320 | tf_op jit(solution)/shard_map/all_gather | solution.py:60
  173.8 17.7 %while.11 = (s32[]{:T(128)}, f32[2,8,8]{2,1,0:T(8,128)S(1)}, bf16[8,64,8,512]{3,2,1,0:T(8,128)(2,1)}, bf16[2,512,512]{2,1,0:T(8,128)(2,1)S(1)}, s32[]{:T(128)}, /*index=5*/s32[]{:T(128)}) while((s32[]{:T(128)}, f32[2,8,8]{2,1,0:T(8,128)S(1)}, bf16[8,64,8,512]{3,2,1,0:T(8,128)(2,1)}, bf16[2,512,512]{2,1,0:T(8,128)(2,1)S(1)}, ...), condition=%wide.region_1.2_spmd.clone, body=%wide.region_0.1_spmd.clone.sunk | while | flops 545784064 | bytes 2099279 | solution.py:34
  173.8 2.2 fusion.31
  176.0 2.2 fusion.31
  178.2 2.2 fusion.31
  180.4 2.2 fusion.31
  182.7 2.2 fusion.31
  184.9 2.2 fusion.31
  187.1 2.2 fusion.31
  189.3 2.2 fusion.31
  191.5 43.0 %all-reduce = f32[2,8,8]{2,0,1:T(2,128)S(1)} all-reduce(f32[2,8,8]{2,0,1:T(2,128)S(1)} %copy.25), channel_id=2, replica_groups=mesh['pair'=64,'aux'=8] {'aux'}, use_global_device_ids=true, to_apply=%region_2.3.clone | all-reduce | flops 128 | bytes 1024
  234.6 1.2 fusion.20
  (11 shorter events, 0.0 us)
Async XLA Ops:
  6.5 1.6 copy-start
  6.5 3.5 %copy-start.1 = (bf16[2,64,512]{2,1,0:T(8,128)(2,1)S(1)}, bf16[2,64,512]{2,1,0:T(8,128)(2,1)}, u32[]{:S(2)}) copy-start(bf16[2,64,512]{2,1,0:T(8,128)(2,1)} %param.9) | copy-start | bytes 393220
  6.5 167.3 %all-gather.2.cloned.1.call-start = ((), (), s32[]{:S(2)}) async-start(), calls=%async_computation.1 | async-start | bytes 4259840 | tf_op jit(solution)/shard_map/all_gather | solution.py:60
  10.0 18.0 %copy-start.5 = (f32[8]{0:T(128)S(1)}, f32[8]{0:T(128)}, u32[]{:S(2)}) copy-start(f32[8]{0:T(128)} %param.14) | copy-start | bytes 100
  10.0 19.8 %copy-start.3 = (s32[2,2]{1,0:T(2,128)S(1)}, s32[2,2]{1,0:T(2,128)}, u32[]{:S(2)}) copy-start(s32[2,2]{1,0:T(2,128)} %param.15) | copy-start | bytes 52
  10.0 20.0 %copy-start.4 = (f32[256]{0:T(256)S(1)}, f32[256]{0:T(256)}, u32[]{:S(2)}) copy-start(f32[256]{0:T(256)} %param.13) | copy-start | bytes 3076
  10.1 20.9 %copy-start.2 = (bf16[256,512]{1,0:T(8,128)(2,1)S(1)}, bf16[256,512]{1,0:T(8,128)(2,1)}, u32[]{:S(2)}) copy-start(bf16[256,512]{1,0:T(8,128)(2,1)} %param.10) | copy-start | bytes 786436
  11.2 75.0 %all-to-all-start = ((bf16[8,2,64,512]{3,2,1,0:T(8,128)(2,1)}), bf16[8,2,64,512]{3,2,1,0:T(8,128)(2,1)S(1)}, u32[]{:S(2)}, u32[]{:S(2)}) async-start(bf16[8,2,64,512]{3,2,1,0:T(8,128)(2,1)} %stack.2), calls=%async_computation | async-start | bytes 2097152 | tf_op jit(solution)/shard_map/all_to_all | solution.py:12
Sparse Core Ops, SparseCore 0:
  10.2 163.5 all-gather.1
